TPU v7x, 256 devices: a whole 4x4x8 slice. The times are simulated.
256 devices in a mesh: item: 64 (over z, y, core), dp: 4 (over x).
Axes of the slice: x: 4, y: 4, z: 8, core: 2. Of those that a mesh axis runs over, the one named last changes fastest.
Arguments:
- query_feats: bfloat16 [4, 1024, 256], P('dp', 'item'), may hold values from -6 to 6
- positives: int32 [4, 1024], P('dp'), may hold values from 0 to 262143
- query_count: int32 [4, 64], P('dp'), may hold values from 1 to 16, as said below
- item_table: bfloat16 [262144, 256], P('item'), may hold values from -6 to 6
- item_gates: float32 [4, 262144], P(None, 'item'), may hold values from -5 to 5
- w_in: bfloat16 [256, 512], replicated, may hold values from -0.375 to 0.375
- w_out: bfloat16 [512, 256], replicated, may hold values from -0.25 to 0.25
- w_gate: bfloat16 [512, 4], replicated, may hold values from -1.25 to 1.25
Outputs:
- grad_feats: float32 [4, 1024, 256], P('dp', 'item')
- grad_w_in: float32 [256, 512], replicated
- grad_w_out: float32 [512, 256], replicated
- grad_w_gate: float32 [512, 4], replicated
Inputs may be any that keep to these rules, and one draw needn't show every extreme that they name: `query_count`: valid queries of a device's slots; the counts of one group sum to at most 768, exactly that in some group, and some device of every group has all 16 slots valid.
All inputs are finite; a program needn't handle non-finite values.
Results may differ from a plain program's by a relative error of at most 0.0053.
Values may be sent and summed in bfloat16 or wider, within the bound.
A program may use at most 64 MiB of HBM per device.

v0:
```python
import jax
import jax.numpy as jnp
from jax import lax
from jax.sharding import PartitionSpec as P

EPS = 1e-06
TAU = 0.05


def unit_rows(raw_vals):
    scale = lax.rsqrt(jnp.sum(raw_vals * raw_vals, axis=-1, keepdims=True) + EPS)
    return (raw_vals * scale, scale)


def gate_weights(gate_logits, reduce_axis):
    exp_terms = jnp.exp(gate_logits)
    return exp_terms / jnp.sum(exp_terms, axis=reduce_axis, keepdims=True)


def item_sweep(query_rows, query_gate, item_norm, item_gates):
    row_count = query_rows.shape[0]
    components = query_rows.shape[1]
    comp_width = query_rows.shape[2]
    item_span = item_norm.shape[0]
    block_len = min(512, item_span)
    block_count = item_span // block_len
    item_blocks = item_norm.reshape(block_count, block_len, components, comp_width)
    gate_blocks = item_gates.reshape(components, block_count, block_len).transpose(1, 0, 2)
    gate_f = query_gate.astype(jnp.float32).T[:, :, None]

    def one_block(state_in, input_block_part):
        totals, update_delta, gate_sum = state_in
        item_part, gate_part = input_block_part
        score_matrix = jnp.einsum(
            "rkd,ikd->kri", query_rows, item_part, preferred_element_type=jnp.float32
        )
        weights = gate_weights(gate_f + gate_part[:, None, :], 0)
        logits = jnp.sum(weights * score_matrix, axis=0) / TAU
        exp_logit = jnp.exp(logits)
        totals = totals + jnp.sum(exp_logit, axis=1)
        coef_bf = (exp_logit[None] * weights / TAU).astype(jnp.bfloat16)
        update_delta = update_delta + jnp.einsum(
            "kri,ikd->rkd", coef_bf, item_part, preferred_element_type=jnp.float32
        )
        gate_sum = (
            gate_sum
            + jnp.sum(exp_logit[None] * weights * (score_matrix - TAU * logits[None]), axis=2) / TAU
        )
        return ((totals, update_delta, gate_sum), None)

    initial = (
        jnp.zeros((row_count,), jnp.float32),
        jnp.zeros((row_count, components, comp_width), jnp.float32),
        jnp.zeros((components, row_count), jnp.float32),
    )
    (totals, update_delta, gate_sum), _ = lax.scan(one_block, initial, (item_blocks, gate_blocks))
    return (totals, update_delta, gate_sum.T)


def positive_terms(query_rows, query_gate, positive, item_norm, item_gates, item_base):
    item_span = item_norm.shape[0]
    local_id = positive - item_base
    inside = (local_id >= 0) & (local_id < item_span)
    safe_id = jnp.clip(local_id, 0, item_span - 1)
    item_pos = jnp.take(item_norm, safe_id, axis=0).astype(jnp.float32)
    gate_pos = jnp.take(item_gates, safe_id, axis=1).T
    query_float_rows = query_rows.astype(jnp.float32)
    score_pos = jnp.sum(query_float_rows * item_pos, axis=-1)
    weight_pos = gate_weights(query_gate.astype(jnp.float32) + gate_pos, 1)
    logit_pos = jnp.sum(weight_pos * score_pos, axis=-1) / TAU
    keep_rows = inside.astype(jnp.float32)
    pos_query = weight_pos[:, :, None] * item_pos / TAU * keep_rows[:, None, None]
    pos_gate = weight_pos * (score_pos - TAU * logit_pos[:, None]) / TAU * keep_rows[:, None]
    return (pos_query, pos_gate)


def per_device(query_feats, positives, query_count, item_table, item_gates, w_in, w_out, w_gate):
    shard_count = lax.axis_size("item")
    item_rank = lax.axis_index("item")
    own_rows = query_feats.shape[1]
    feat_width = query_feats.shape[2]
    components = w_gate.shape[1]
    emb_width = w_out.shape[1]
    comp_width = emb_width // components
    slot_total = own_rows * shard_count
    features = query_feats[0]
    counts = query_count[0]
    preact = jnp.dot(features, w_in, preferred_element_type=jnp.float32)
    hidden = jax.nn.silu(preact).astype(jnp.bfloat16)
    query_raw = jnp.dot(hidden, w_out, preferred_element_type=jnp.float32).reshape(
        own_rows, components, comp_width
    )
    query_gate = jnp.dot(hidden, w_gate, preferred_element_type=jnp.float32).astype(jnp.bfloat16)
    query_unit, query_scale = unit_rows(query_raw)
    query_norm = query_unit.astype(jnp.bfloat16).reshape(own_rows, emb_width)
    all_query, all_gate = (
        lax.all_gather(query_norm, "item", axis=0, tiled=True),
        lax.all_gather(query_gate, "item", axis=0, tiled=True),
    )
    item_span = item_table.shape[0]
    item_norm = unit_rows(
        item_table.astype(jnp.float32).reshape(item_span, components, comp_width)
    )[0].astype(jnp.bfloat16)
    slot_in_dev = jnp.arange(own_rows, dtype=jnp.int32)
    valid_slot = (slot_in_dev[None, :] < counts[:, None]).reshape(slot_total)
    item_base = item_rank * item_span
    group_position = positives[0]
    query_rows = all_query.reshape(-1, components, comp_width)
    totals, update_delta, gate_sum = item_sweep(query_rows, all_gate, item_norm, item_gates)
    pos_query, pos_gate = positive_terms(
        query_rows, all_gate, group_position, item_norm, item_gates, item_base
    )
    live_f = valid_slot.astype(jnp.float32)
    totals_all = lax.psum(totals, "item")
    query_term_part = (update_delta / totals_all[:, None, None] - pos_query) * live_f[:, None, None]
    term_gate = (gate_sum / totals_all[:, None] - pos_gate) * live_f[:, None]
    grad_query, grad_gate = (
        lax.psum_scatter(
            query_term_part.reshape(slot_total, emb_width), "item", scatter_dimension=0, tiled=True
        ),
        lax.psum_scatter(term_gate, "item", scatter_dimension=0, tiled=True),
    )
    grad_query = grad_query.reshape(own_rows, components, comp_width)
    dot_sum = jnp.sum(grad_query * query_raw, axis=-1, keepdims=True)
    grad_raw = (query_scale * grad_query - query_raw * query_scale**3 * dot_sum).reshape(
        own_rows, emb_width
    )
    highest = lax.Precision.HIGHEST
    grad_hidden = jnp.dot(grad_raw, w_out.astype(jnp.float32).T, precision=highest) + jnp.dot(
        grad_gate, w_gate.astype(jnp.float32).T, precision=highest
    )
    sigmoid_pre = jax.nn.sigmoid(preact)
    grad_preact = grad_hidden * sigmoid_pre * (1.0 + preact * (1.0 - sigmoid_pre))
    grad_feats = jnp.dot(grad_preact, w_in.astype(jnp.float32).T, precision=highest).reshape(
        1, own_rows, feat_width
    )
    hidden_f = hidden.astype(jnp.float32)
    part_in = jnp.dot(features.astype(jnp.float32).T, grad_preact, precision=highest)
    part_out = jnp.dot(hidden_f.T, grad_raw, precision=highest)
    part_gate = jnp.dot(hidden_f.T, grad_gate, precision=highest)
    grad_w_in, grad_w_out, grad_w_gate = lax.psum((part_in, part_out, part_gate), ("item", "dp"))
    return (grad_feats, grad_w_in, grad_w_out, grad_w_gate)


def solution(mesh):
    in_specs = (
        P("dp", "item", None),
        P("dp", None),
        P("dp", None),
        P("item", None),
        P(None, "item"),
        P(),
        P(),
        P(),
    )
    out_specs = (P("dp", "item", None), P(), P(), P())
    return jax.shard_map(
        per_device, mesh=mesh, in_specs=in_specs, out_specs=out_specs, check_vma=False
    )
```

profile of v0, /device:TPU:1, one launch (start us, length us, event | category | flops | bytes accessed | tf_op | source)
XLA Modules:
  0.0 914.2 jit_solution(16929554966947675786)
XLA Ops:
  16.9 54.9 %all_gather.7 = bf16[1024,256]{1,0:T(8,128)(2,1)S(1)} all-gather(bf16[16,256]{1,0:T(8,128)(2,1)S(1)} %multiply_convert_fusion.9), channel_id=1, replica_groups=mesh['item'=64,'dp'=4] {'item'}, dimensions={0}, use_global_device_ids=true | all-gather | bytes 532480 | tf_op jit(solution)/shard_map/all_gather | solution.py:97
  74.7 7.0 copy.75
  81.7 5.7 gather_fusion.1
  88.8 42.9 %all-gather = bf16[64,16,4]{1,2,0:T(4,128)(2,1)S(1)} all-gather(bf16[1,16,4]{1,2,0:T(4,128)(2,1)S(1)} %fusion.19), channel_id=1, replica_groups=mesh['item'=64,'dp'=4] {'item'}, dimensions={0}, use_global_device_ids=true | all-gather | bytes 8320 | tf_op jit(solution)/shard_map/all_gather | solution.py:98
  133.4 4.4 gather_fusion
  139.1 6.0 copy.81
  148.6 118.4 %while.17 = (s32[]{:T(128)}, f32[1024]{0:T(1024)S(1)}, f32[1024,4,64]{0,2,1:T(8,128)}, f32[4,1024]{1,0:T(4,128)S(1)}, f32[4,1024,1]{1,0,2:T(4,128)S(1)}, /*index...) while((s32[]{:T(128)}, f32[1024]{0:T(1024)S(1)}, ...), condition=%wide.region_7.8_spmd.clone, body=%wide.region_2.7_spmd.clone.sunk | while | flops 573056000 | bytes 49480844 | solution.py:56
  150.7 4.1 fusion.63
  158.2 5.0 fusion.64
  165.3 4.1 fusion.63
  172.7 5.3 fusion.64
  180.1 4.1 fusion.63
  187.6 5.3 fusion.64
  202.4 5.3 fusion.64
  209.8 4.1 fusion.63
  217.2 5.3 fusion.64
  232.0 5.3 fusion.64
  239.4 4.1 fusion.63
  246.9 5.3 fusion.64
  261.7 5.3 fusion.64
  267.0 123.7 %psum.28 = f32[1024]{0:T(1024)S(1)} all-reduce(f32[1024]{0:T(1024)S(1)} %get-tuple-element.108), channel_id=1, replica_groups=mesh['item'=64,'dp'=4] {'item'}, use_global_device_ids=true, to_apply=%region_8.9 | all-reduce | flops 1024 | bytes 8192 | tf_op jit(solution)/shard_map/psum | solution.py:114
  396.3 246.7 %all-reduce = f32[1024,4]{1,0:T(8,128)S(1)} all-reduce(f32[1024,4]{1,0:T(8,128)S(1)} %copy.78), channel_id=3, replica_groups=mesh['item'=64,'dp'=4] {'item'}, use_global_device_ids=true, to_apply=%region_14.15.clone | all-reduce | flops 4096 | bytes 32768
  647.9 78.8 %psum.31 = f32[512,4]{0,1:T(4,128)} all-reduce(f32[512,4]{0,1:T(4,128)S(1)} %fusion.30), channel_id=1, replica_groups=mesh['item'=64,'dp'=4] {'item','dp'}, use_global_device_ids=true, to_apply=%region_17.18 | all-reduce | flops 2048 | bytes 16384 | tf_op jit(solution)/shard_map/psum | solution.py:141
  727.6 175.8 %all-reduce.4.cloned.1.call-done = (f32[256,512]{0,1:T(8,128)}, f32[512,256]{1,0:T(8,128)}) async-done(((f32[256,512]{0,1:T(8,128)}, f32[512,256]{1,0:T(8,128)}), (f32[256,512]{0,1:T(8,128)}, f32[512,256]{1,0:T(8,128)})) %all-reduce.4.cloned.1.call-update) | async-done | bytes 1048592 | tf_op jit(solution)/shard_map/psum | solution.py:141
  (169 shorter events, 90.9 us)
Async XLA Ops:
  7.2 7.3 copy-start
  7.2 635.8 %reduce-scatter.2.cloned.1.call-start = ((), (), s32[]{:S(2)}) async-start(), calls=%async_computation.1 | async-start | bytes 1064960 | tf_op jit(solution)/shard_map/reduce_scatter | solution.py:118
  10.2 5.0 copy-start.2
  74.7 13.9 %copy-start.18 = (bf16[512,4]{0,1:T(4,128)(2,1)S(1)}, bf16[512,4]{0,1:T(4,128)(2,1)}, u32[]{:S(2)}) copy-start(bf16[512,4]{0,1:T(4,128)(2,1)} %param.17) | copy-start | bytes 12292
  81.7 7.1 copy-start.10
  139.0 8.9 copy-start.5
  148.6 242.2 %copy-start.17 = (s32[1,64]{1,0:T(1,128)S(1)}, s32[1,64]{1,0:T(1,128)}, u32[]{:S(2)}) copy-start(s32[1,64]{1,0:T(1,128)} %param.12) | copy-start | bytes 772
  148.6 242.3 %copy-start.6 = (f32[1024,4]{0,1:T(4,128)S(1)}, f32[1024,4]{0,1:T(4,128)}, u32[]{:S(2)}) copy-start(f32[1024,4]{0,1:T(4,128)} %copy-done.5) | copy-start | bytes 49156
  150.7 4.4 copy-start.1
  165.3 4.4 copy-start.1
  180.1 4.4 copy-start.1
  194.9 4.4 copy-start.1
  209.8 4.4 copy-start.1
  224.6 4.4 copy-start.1
  239.4 4.4 copy-start.1
  267.0 127.6 %copy-start.9 = (f32[1,1024]{1,0:T(1,128)S(1)}, f32[1,1024]{1,0:T(1,128)}, u32[]{:S(2)}) copy-start(f32[1,1024]{1,0:T(1,128)} %and_select_fusion) | copy-start | bytes 12292
  267.0 127.9 %copy-start.14 = (f32[16,4]{1,0:T(8,128)S(1)}, f32[16,4]{1,0:T(8,128)}, u32[]{:S(2)}) copy-start(f32[16,4]{1,0:T(8,128)} %get-tuple-element.223) | copy-start | bytes 772
  267.0 128.0 %copy-start.20 = (u32[256]{0:T(256)S(1)}, u32[256]{0:T(256)}, u32[]{:S(2)}) copy-start(u32[256]{0:T(256)} %constant.108) | copy-start | bytes 3076
  267.0 377.0 %copy-start.8 = (f32[16,256]{1,0:T(8,128)S(1)}, f32[16,256]{1,0:T(8,128)}, u32[]{:S(2)}) copy-start(f32[16,256]{1,0:T(8,128)} %copy-done.7) | copy-start | bytes 49156
  267.0 377.8 %copy-start.3 = (bf16[512,256]{1,0:T(8,128)(2,1)S(1)}, bf16[512,256]{1,0:T(8,128)(2,1)}, u32[]{:S(2)}) copy-start(bf16[512,256]{1,0:T(8,128)(2,1)} %param.16) | copy-start | bytes 786436
  391.6 254.7 %copy-start.13 = (f32[16,512]{1,0:T(8,128)S(1)}, f32[16,512]{1,0:T(8,128)}, u32[]{:S(2)}) copy-start(f32[16,512]{1,0:T(8,128)} %get-tuple-element.226) | copy-start | bytes 98308
  391.6 254.7 %copy-start.19 = (bf16[512,4]{0,1:T(4,128)(2,1)S(1)}, bf16[512,4]{0,1:T(4,128)(2,1)}, u32[]{:S(2)}) copy-start(bf16[512,4]{0,1:T(4,128)(2,1)} %param.17) | copy-start | bytes 12292
  391.6 254.8 %copy-start.12 = (bf16[1,16,256]{2,1,0:T(8,128)(2,1)S(1)}, bf16[1,16,256]{2,1,0:T(8,128)(2,1)}, u32[]{:S(2)}) copy-start(bf16[1,16,256]{2,1,0:T(8,128)(2,1)} %param.10) | copy-start | bytes 24580
  394.5 508.9 %all-reduce.4.cloned.1.call-start = ((), (), s32[]{:S(2)}) async-start(), calls=%async_computation.2 | async-start | bytes 2097152 | tf_op jit(solution)/shard_map/psum | solution.py:141
  (6 other events, 18.4 us)
Sparse Core Ops, SparseCore 0:
  394.6 132.7 reduce-scatter.1
  647.8 255.5 all-reduce.3
where the time goes:
time: 916 us; the launch traced here: 914 us
  blocking collectives  547 us (60%)
  waiting for transfers between devices  176 us (19%)
  matrix products  79.4 us (9%)
  other arithmetic  51.5 us (6%)
  local copies, waits for them, and re-layouts  45 us (5%)
  between operations  15 us (2%)
    unnamed x1, blocking collectives  247 us
    psum x1, waiting for transfers between devices, per_device(): lax.psum((part_in, part_out, part_gate), ('item', 'dp'))  176 us
    psum x1, blocking collectives, per_device(): totals_all = lax.psum(totals, 'item')  124 us
    psum x1, blocking collectives, per_device(): lax.psum((part_in, part_out, part_gate), ('item', 'dp'))  78.8 us
    all_gather x1, blocking collectives, per_device(): lax.all_gather(query_norm, 'item', axis=0, tiled=True)  54.9 us
    all_gather x1, blocking collectives, per_device(): lax.all_gather(query_gate, 'item', axis=0, tiled=True)  42.9 us
    dot_general x8, matrix products, one_block(): jnp.einsum('kri,ikd->rkd', coef_bf, item_part, preferred_element_type=jnp...  41.9 us
    dot_general x8, matrix products, one_block(): jnp.einsum('rkd,ikd->kri', query_rows, item_part, preferred_element_type=...  32.5 us
  transfers between devices with their start and end apart: 2, of which 1 were waited for; matrix products, arithmetic and copies ran while one was open for 0% of the time, Pallas kernels for 0%

commit v1 on v0

v1 whole, which is shorter than its diff:
```python
import functools
import math

import jax
import jax.numpy as jnp
from jax import lax
from jax.experimental import pallas as pl
from jax.experimental.pallas import tpu as pltpu
from jax.sharding import PartitionSpec as P

EPS = 1e-06
TAU = 0.05
LOG2E = math.log2(math.e)
LN2 = math.log(2.0)
LANES = 128
CHUNK = 24
PAY = 56
F32 = jnp.float32
BF16 = jnp.bfloat16
MESH = pl.DeviceIdType.MESH


def mm(a, b):
    return lax.dot_general(a, b, (((1,), (0,)), ((), ())), preferred_element_type=F32)


def mm_nt(a, b):
    return lax.dot_general(a, b, (((1,), (1,)), ((), ())), preferred_element_type=F32)


def mm_tn(a, b):
    return lax.dot_general(a, b, (((0,), (0,)), ((), ())), preferred_element_type=F32)


def parts(x, n):
    out = []
    for step in range(n):
        hi = x.astype(BF16)
        out.append(hi)
        if step < n - 1:
            x = x - hi.astype(F32)
    return out


def mmx(x, b, n):
    total = None
    for part in parts(x, n):
        prod = mm(part, b)
        total = prod if total is None else total + prod
    return total


def iota(shape, dim):
    return lax.broadcasted_iota(jnp.int32, shape, dim)


def onehot(cond):
    return jnp.where(cond, 1.0, 0.0).astype(BF16)


def comp_spread(rows, comps, width):
    per = width // comps
    shape = (rows, width)
    return onehot(iota(shape, 0) == iota(shape, 1) // per)


def comp_fold(width, comps):
    per = width // comps
    shape = (width, LANES)
    return onehot(iota(shape, 0) // per == iota(shape, 1))


def comp_block(width, comps):
    per = width // comps
    shape = (width, width)
    return onehot(iota(shape, 0) // per == iota(shape, 1) // per)


def place(n_y, n_z):
    me = lax.axis_index("item")
    core = lax.rem(me, 2)
    y = lax.rem(me // 2, n_y)
    z = me // (2 * n_y)
    return core, y, z


def item_id(core, y, z, n_y):
    return (z * n_y + y) * 2 + core


def remote(src, dst, send, recv, item, dp):
    return pltpu.make_async_remote_copy(
        src_ref=src,
        dst_ref=dst,
        send_sem=send,
        recv_sem=recv,
        device_id=(item, dp),
        device_id_type=MESH,
    )


def greet(peers):
    barrier = pltpu.get_barrier_semaphore()
    for item, dp in peers:
        pl.semaphore_signal(barrier, inc=1, device_id=(item, dp), device_id_type=MESH)
    pl.semaphore_wait(barrier, len(peers))


def item_peers(core, y, z, n_y, n_z, dp):
    z_peers = [(item_id(core, y, lax.rem(z + s, n_z), n_y), dp) for s in range(1, n_z)]
    y_peers = [(item_id(core, lax.rem(y + s, n_y), z, n_y), dp) for s in range(1, n_y)]
    partner = (item_id(1 - core, y, z, n_y), dp)
    return z_peers, y_peers, partner


def spread_blocks(buf, core, y, z, peers, sems):
    z_peers, y_peers, partner = peers
    zs, zr, ys, yr, cs, cr = sems
    copies = []
    for s, (item, dp) in enumerate(z_peers):
        block = buf.at[core, y, z]
        copies.append(remote(block, block, zs.at[s], zr.at[s], item, dp))
        copies[-1].start()
    for copy in copies:
        copy.wait()
    copies = []
    for s, (item, dp) in enumerate(y_peers):
        block = buf.at[core, y]
        copies.append(remote(block, block, ys.at[s], yr.at[s], item, dp))
        copies[-1].start()
    for copy in copies:
        copy.wait()
    block = buf.at[core]
    copy = remote(block, block, cs, cr, partner[0], partner[1])
    copy.start()
    copy.wait()


def gather_sems(n_y, n_z):
    dma = pltpu.SemaphoreType.DMA
    return [dma((n_z - 1,)), dma((n_z - 1,)), dma((n_y - 1,)), dma((n_y - 1,)), dma(()), dma(())]


def gather_kernel(n_y, n_z, x_ref, o_ref, local_sem, *sems):
    core, y, z = place(n_y, n_z)
    dp = lax.axis_index("dp")
    peers = item_peers(core, y, z, n_y, n_z, dp)
    mine = pltpu.make_async_copy(x_ref, o_ref.at[core, y, z], local_sem)
    mine.start()
    greet(peers[0] + peers[1] + [peers[2]])
    mine.wait()
    spread_blocks(o_ref, core, y, z, peers, sems)


def gather_rows(x, n_y, n_z):
    return pl.pallas_call(
        functools.partial(gather_kernel, n_y, n_z),
        out_shape=jax.ShapeDtypeStruct((2, n_y, n_z) + x.shape, x.dtype),
        in_specs=[pl.BlockSpec(memory_space=pltpu.VMEM)],
        out_specs=pl.BlockSpec(memory_space=pltpu.VMEM),
        scratch_shapes=[pltpu.SemaphoreType.DMA(())] + gather_sems(n_y, n_z),
        compiler_params=pltpu.CompilerParams(collective_id=0, has_side_effects=True),
        name="gather_rows",
    )(x)


def query_tower(x, w_in, w_out, w_gate):
    pre = mm(x, w_in)
    hid = (pre * jax.nn.sigmoid(pre)).astype(BF16)
    raw = mm(hid, w_out)
    gate = mm(hid, w_gate).astype(BF16).astype(F32)
    return pre, hid, raw, gate


def sweep_kernel(
    comps,
    x_ref,
    rank_ref,
    pos_ref,
    tab_ref,
    gate_ref,
    w_in_ref,
    w_out_ref,
    w_gate_ref,
    pay_ref,
    qb_ref,
    xc_ref,
    pre_ref,
    hid_ref,
    raw_ref,
    scaled_ref,
    normed_ref,
    ei_den,
    ei_sum,
    q_ref,
    qn_ref,
    eq_ref,
    eqb_ref,
    posc_ref,
    acc,
    pos_acc,
    tot_acc,
    g_acc,
    p_acc,
    sc_ref,
):
    rows, emb = q_ref.shape
    items = tab_ref.shape[0]
    slots = x_ref.shape[0]
    rb = 256 if rows % 256 == 0 else rows
    it = 512 if items % 512 == 0 else items
    spread = comp_spread(LANES, comps, emb)
    fold = comp_fold(emb, comps)
    block = comp_block(emb, comps)
    lane_shape = (rb, LANES)
    is_comp = iota(lane_shape, 1) < comps

    spread16 = onehot(
        (iota((16, emb), 0) % 4 == iota((16, emb), 1) // (emb // comps)) & (iota((16, emb), 0) < 12)
    )

    @pl.loop(0, items // it)
    def _(t):
        sl = pl.ds(pl.multiple_of(t * it, it), it)
        tab = tab_ref[sl, :].astype(F32)
        norm = (tab * lax.rsqrt(mmx(tab * tab, block, 2) + EPS)).astype(BF16)
        normed_ref[sl, :] = norm
        ei = jnp.exp(gate_ref[:, sl])
        hi, lo, lo2 = parts(ei, 3)
        row = iota(ei.shape, 0)
        zero = jnp.zeros_like(ei)
        hi, lo, lo2 = hi.astype(F32), lo.astype(F32), lo2.astype(F32)
        ei_den[:, sl] = jnp.where(row < 8, hi, jnp.where(row < 12, lo, zero)).astype(BF16)
        ei_sum[:, sl] = jnp.where(row < 4, hi, jnp.where(row < 8, lo, zero)).astype(BF16)
        ei_all = jnp.where(row < 4, hi, jnp.where(row < 8, lo, jnp.where(row < 12, lo2, zero))).astype(BF16)
        factor = mm_tn(ei_all, spread16)
        scaled_ref[sl, :] = (norm.astype(F32) * factor).astype(BF16)

    shift_a = onehot(
        ((iota((LANES, 16), 1) == iota((LANES, 16), 0)) | (iota((LANES, 16), 1) == iota((LANES, 16), 0) + 8))
        & (iota((LANES, 16), 0) < 4)
    )
    shift_b = onehot((iota((LANES, 16), 1) == iota((LANES, 16), 0) + 4) & (iota((LANES, 16), 0) < 4))
    for r in range(rows // rb):
        rs = slice(r * rb, (r + 1) * rb)
        picked = iota((rb, slots), 0) + r * rb == rank_ref[...]
        xc = mm(onehot(picked), x_ref[...]).astype(BF16)
        posc_ref[rs, :] = jnp.sum(jnp.where(picked, pos_ref[...], 0.0), axis=1, keepdims=True)
        pre, hid, raw, gate = query_tower(xc, w_in_ref[...], w_out_ref[...], w_gate_ref[...])
        xc_ref[rs, :] = xc
        pre_ref[rs, :] = pre
        hid_ref[rs, :] = hid
        raw_ref[rs, :] = raw
        qn = (raw * lax.rsqrt(mmx(raw * raw, block, 3) + EPS)).astype(BF16)
        qn_ref[rs, :] = qn
        top = jnp.max(jnp.where(is_comp, gate, -3.0e38), axis=1, keepdims=True)
        eq = jnp.where(is_comp, jnp.exp(gate - top), 0.0)
        eqb = mmx(eq, spread, 3)
        eqb_ref[rs, :] = eqb
        q_ref[rs, :] = (qn.astype(F32) * (eqb * (LOG2E / TAU))).astype(BF16)
        hi, lo = parts(eq, 2)
        eq_ref[rs, :] = (mm(hi, shift_a) + mm(lo, shift_b)).astype(BF16)

    acc[...] = jnp.zeros_like(acc)
    pos_acc[...] = jnp.zeros_like(pos_acc)
    tot_acc[...] = jnp.zeros_like(tot_acc)
    g_acc[...] = jnp.zeros_like(g_acc)
    p_acc[...] = jnp.zeros_like(p_acc)

    @pl.loop(0, items // it)
    def _(t):
        sl = pl.ds(pl.multiple_of(t * it, it), it)
        local = iota((rb, it), 1) + t * it
        for r in range(rows // rb):
            rs = slice(r * rb, (r + 1) * rb)
            num = mm_nt(q_ref[rs, :], scaled_ref[sl, :])
            den = mm(eq_ref[rs, :], ei_den[:, sl])
            inv = 1.0 / den
            log2_expo = num * inv
            expo = jnp.exp2(log2_expo)
            coef = expo * inv
            tot_acc[rs, :] += jnp.sum(expo, axis=1, keepdims=True)
            acc[rs, :] += mm(coef.astype(BF16), scaled_ref[sl, :])
            g_acc[rs, :] += mm_nt((coef * log2_expo).astype(BF16), ei_sum[:, sl])
            here = onehot(posc_ref[rs, :].astype(jnp.int32) == local)
            pos_acc[rs, :] += mm(here, normed_ref[sl, :])
            p_acc[rs, :] += mm_nt(here, ei_sum[:, sl])

    fold16 = onehot((iota((16, LANES), 0) % 4 == iota((16, LANES), 1)) & (iota((16, LANES), 0) < 8))
    ll = (LANES, LANES)
    spot = 8 * (iota(ll, 0) // 2) + iota(ll, 0) % 2
    to_g, to_hi, to_lo = (onehot((iota(ll, 1) == spot + j) & (iota(ll, 0) < comps)) for j in (2, 4, 6))
    lane = iota(lane_shape, 1)
    for r in range(rows // rb):
        rs = slice(r * rb, (r + 1) * rb)
        eqb = eqb_ref[rs, :]
        acc[rs, :] = acc[rs, :] * eqb * (1.0 / TAU)
        eq = mmx(eq_ref[rs, :].astype(F32), fold16, 1)
        second = eq * mmx(g_acc[rs, :], fold16, 3) * LN2
        weight = eq * mmx(p_acc[rs, :], fold16, 3)
        weight_sum = jnp.sum(weight, axis=1, keepdims=True)
        weight = weight / jnp.where(weight_sum > 0.0, weight_sum, 1.0)
        pos_item = pos_acc[rs, :]
        score = mmx(qn_ref[rs, :].astype(F32) * pos_item, fold, 3)
        logit = jnp.sum(weight * score, axis=1, keepdims=True) / TAU
        pos_acc[rs, :] = mmx(weight, spread, 3) * pos_item * (1.0 / TAU)
        tot_hi, tot_lo = parts(tot_acc[rs, :], 2)
        scalars = jnp.where(lane % 8 == 0, tot_hi.astype(F32), jnp.where(lane % 8 == 1, tot_lo.astype(F32), 0.0))
        pg_hi, pg_lo = parts(weight * (score * (1.0 / TAU) - logit), 2)
        scalars = scalars + mmx(second, to_g, 1) + mm(pg_hi, to_hi) + mm(pg_lo, to_lo)
        sc_ref[rs, :] = scalars.astype(BF16)
    sc_ref[rows:, :] = jnp.zeros((LANES, LANES), BF16)

    n_y, n_z = pay_ref.shape[1:3]
    eye = onehot(iota((16, LANES), 0) == iota((16, LANES), 1))
    for b in range(n_y * n_z):
        y, z = b // n_z, b % n_z
        rs = slice(b * CHUNK, (b + 1) * CHUNK)
        scalars = mm_nt(eye, sc_ref[b * CHUNK : b * CHUNK + LANES, :])
        for c in range(2):
            cols = slice(c * LANES, (c + 1) * LANES)
            pay_ref[c, y, z, 0:CHUNK, :] = acc[rs, cols].astype(BF16)
            pay_ref[c, y, z, CHUNK : 2 * CHUNK, :] = pos_acc[rs, cols].astype(BF16)
            pay_ref[c, y, z, 2 * CHUNK : PAY, :] = scalars[c * 8 : c * 8 + 8, :].astype(BF16)
            qb_ref[c, y, z] = qn_ref[rs, cols]


def sweep(x_all, ranks, pos_local, table, gates16, w_in, w_out, w_gate, comps, rows, n_y, n_z):
    emb, hid = w_out.shape[1], w_out.shape[0]
    items = table.shape[0]
    vmem = pl.BlockSpec(memory_space=pltpu.VMEM)
    sds = jax.ShapeDtypeStruct
    return pl.pallas_call(
        functools.partial(sweep_kernel, comps),
        out_shape=(
            sds((2, n_y, n_z, PAY, LANES), BF16),
            sds((2, n_y, n_z, CHUNK, LANES), BF16),
            sds((rows, x_all.shape[1]), BF16),
            sds((rows, hid), F32),
            sds((rows, hid), BF16),
            sds((rows, emb), F32),
        ),
        in_specs=[vmem] * 8,
        out_specs=(vmem,) * 6,
        scratch_shapes=[
            pltpu.VMEM((items, emb), BF16),
            pltpu.VMEM((items, emb), BF16),
            pltpu.VMEM((16, items), BF16),
            pltpu.VMEM((16, items), BF16),
            pltpu.VMEM((rows, emb), BF16),
            pltpu.VMEM((rows, emb), BF16),
            pltpu.VMEM((rows, 16), BF16),
            pltpu.VMEM((rows, emb), F32),
            pltpu.VMEM((rows, 1), F32),
            pltpu.VMEM((rows, emb), F32),
            pltpu.VMEM((rows, emb), F32),
            pltpu.VMEM((rows, 1), F32),
            pltpu.VMEM((rows, 16), F32),
            pltpu.VMEM((rows, 16), F32),
            pltpu.VMEM((rows + LANES, LANES), BF16),
        ],
        compiler_params=pltpu.CompilerParams(vmem_limit_bytes=56 * 1024 * 1024),
        name="sweep",
    )(x_all, ranks, pos_local, table, gates16, w_in, w_out, w_gate)


def reduce_kernel(n_y, n_z, pay_ref, qb_ref, o_ref, in_c, acc_c, in_y, acc_y, in_z, *sems):
    core, y, z = place(n_y, n_z)
    dp = lax.axis_index("dp")
    peers = item_peers(core, y, z, n_y, n_z, dp)
    z_peers, y_peers, partner = peers
    cs, cr, ys, yr, zs, zr = sems[:6]
    greet(z_peers + y_peers + [partner])

    copy = remote(pay_ref.at[1 - core], in_c, cs, cr, partner[0], partner[1])
    copy.start()
    copy.wait()
    for j in range(n_y):
        acc_c[j] = (pay_ref[core, j].astype(F32) + in_c[j].astype(F32)).astype(BF16)

    copies = []
    for s, (item, _) in enumerate(y_peers):
        target = lax.rem(y + s + 1, n_y)
        copies.append(remote(acc_c.at[target], in_y.at[s], ys.at[s], yr.at[s], item, dp))
        copies[-1].start()
    for copy in copies:
        copy.wait()
    total = acc_c[y].astype(F32)
    for s in range(n_y - 1):
        total = total + in_y[s].astype(F32)
    acc_y[...] = total.astype(BF16)

    copies = []
    for s, (item, _) in enumerate(z_peers):
        target = lax.rem(z + s + 1, n_z)
        copies.append(remote(acc_y.at[target], in_z.at[s], zs.at[s], zr.at[s], item, dp))
        copies[-1].start()
    for copy in copies:
        copy.wait()
    total = acc_y[z].astype(F32)
    for s in range(n_z - 1):
        total = total + in_z[s].astype(F32)

    update, positive, scal = total[0:CHUNK], total[CHUNK : 2 * CHUNK], total[2 * CHUNK : PAY]
    lane = iota((8, LANES), 1)
    row = iota((8, LANES), 0)
    soft_row = jnp.where(lane[0:1] < CHUNK, scal[0:1] + scal[1:2], 1.0)
    diag = iota((CHUNK, LANES), 0) == iota((CHUNK, LANES), 1)
    soft_col = jnp.sum(jnp.where(diag, soft_row, 0.0), axis=1, keepdims=True)
    inner = qb_ref[core, y, z].astype(F32) * update
    inner = jnp.concatenate([inner, jnp.zeros((LANES - CHUNK, LANES), F32)], axis=0)
    select = onehot(row == lane // (LANES // 2) + 2)
    first = sum(mm_nt(select, part) for part in parts(inner, 3))
    gate = (first - scal) / soft_row - pltpu.roll(scal, 6, 0) - pltpu.roll(scal, 4, 0)
    gate = jnp.where((row >= 2) & (row < 4) & (lane < CHUNK), gate, 0.0)
    hi = gate.astype(BF16).astype(F32)
    low = pltpu.roll(gate - hi, 2, 0)
    o_ref[core, y, z, 0:CHUNK, :] = (update / soft_col - positive).astype(BF16)
    o_ref[core, y, z, CHUNK : CHUNK + 8, :] = (hi + low).astype(BF16)
    spread_blocks(o_ref, core, y, z, peers, sems[6:])


def reduce_rows(pay, qb, n_y, n_z):
    vmem = pl.BlockSpec(memory_space=pltpu.VMEM)
    dma = pltpu.SemaphoreType.DMA
    block = (PAY, LANES)
    return pl.pallas_call(
        functools.partial(reduce_kernel, n_y, n_z),
        out_shape=jax.ShapeDtypeStruct((2, n_y, n_z, CHUNK + 8, LANES), BF16),
        in_specs=[vmem] * 2,
        out_specs=vmem,
        scratch_shapes=[
            pltpu.VMEM((n_y, n_z) + block, BF16),
            pltpu.VMEM((n_y, n_z) + block, BF16),
            pltpu.VMEM((n_y - 1, n_z) + block, BF16),
            pltpu.VMEM((n_z,) + block, BF16),
            pltpu.VMEM((n_z - 1,) + block, BF16),
            dma(()),
            dma(()),
            dma((n_y - 1,)),
            dma((n_y - 1,)),
            dma((n_z - 1,)),
            dma((n_z - 1,)),
        ]
        + gather_sems(n_y, n_z),
        compiler_params=pltpu.CompilerParams(
            collective_id=1, has_side_effects=True, vmem_limit_bytes=32 * 1024 * 1024
        ),
        name="reduce_rows",
    )(pay, qb)


def backward_kernel(
    comps,
    own_ref,
    g_ref,
    xc_ref,
    pre_ref,
    hid_ref,
    raw_ref,
    w_in_ref,
    w_out_ref,
    w_gate_ref,
    stack_ref,
    gate_ref,
    feats_ref,
    gq_ref,
    vv_ref,
):
    rows, emb = raw_ref.shape
    n_y, n_z = g_ref.shape[1:3]
    blocks = n_y * n_z
    for b in range(blocks):
        y, z = b // n_z, b % n_z
        for c in range(2):
            gq_ref[b * CHUNK : (b + 1) * CHUNK, c * LANES : (c + 1) * LANES] = g_ref[c, y, z, 0:CHUNK, :]
            at = (c * blocks + b) * 8
            vv_ref[at : at + 8, :] = g_ref[c, y, z, CHUNK : CHUNK + 8, :]

    width = blocks * 16
    eye = onehot(iota((32, LANES), 0) == iota((32, LANES), 1))
    spots = mm_nt(eye, vv_ref[...]).astype(BF16)
    repeat = onehot(iota((rows, 32), 0) % CHUNK == iota((rows, 32), 1))
    wide = mm(repeat, spots)
    wide = jnp.where(iota((rows, width), 0) // CHUNK == iota((rows, width), 1) // 8 % blocks, wide, 0.0).astype(BF16)
    at_w = iota((width, LANES), 0)
    lane_w = iota((width, LANES), 1) - 2 * (at_w // (8 * blocks))
    kind = at_w % 8
    collect = onehot(((kind == lane_w + 2) | (kind == lane_w + 4)) & (lane_w >= 0) & (lane_w < 2))
    gate = mm(wide, collect)

    block = comp_block(emb, comps)
    gq = gq_ref[...].astype(F32)
    raw = raw_ref[...]
    scale = lax.rsqrt(mmx(raw * raw, block, 3) + EPS)
    dot_sum = mmx(gq * raw, block, 3)
    g_raw = scale * gq - raw * (scale * scale * scale) * dot_sum
    raw_hi, raw_lo = parts(g_raw, 2)
    gate_hi, gate_lo = parts(gate, 2)
    w_out = w_out_ref[...]
    w_gate = w_gate_ref[...]
    g_hid = mm_nt(raw_hi, w_out) + mm_nt(raw_lo, w_out) + mm_nt(gate_hi, w_gate) + mm_nt(gate_lo, w_gate)
    pre = pre_ref[...]
    sig = jax.nn.sigmoid(pre)
    g_pre = g_hid * sig * (1.0 + pre * (1.0 - sig))
    pre_hi, pre_lo = parts(g_pre, 2)

    xc = xc_ref[...]
    hid = hid_ref[...]
    g_in = mm_tn(xc, pre_hi) + mm_tn(xc, pre_lo)
    feat_w = xc.shape[1]
    n_in = g_in.shape[1] // emb
    for j in range(n_in):
        stack_ref[j * feat_w : (j + 1) * feat_w, :] = g_in[:, j * emb : (j + 1) * emb].astype(BF16)
    stack_ref[n_in * feat_w :, :] = (mm_tn(hid, raw_hi) + mm_tn(hid, raw_lo)).astype(BF16)
    gate_ref[...] = (mm_tn(gate_hi, hid) + mm_tn(gate_lo, hid))[0:8, :]

    own = feats_ref.shape[0]
    slot = iota((own, rows), 0)
    take = onehot((iota((own, rows), 1) == slot + own_ref[0]) & (slot < own_ref[1]))
    mine = mm(take, pre_hi) + mm(take, pre_lo)
    feats_ref[...] = sum(mm_nt(part, w_in_ref[...]) for part in parts(mine, 3))


def backward(own, g_all, xc, pre, hid, raw, w_in, w_out, w_gate, comps, own_rows):
    vmem = pl.BlockSpec(memory_space=pltpu.VMEM)
    sds = jax.ShapeDtypeStruct
    rows, emb = raw.shape
    feat_w, hid_w = w_in.shape
    n_y, n_z = g_all.shape[1:3]
    stack_rows = feat_w * (hid_w // emb) + hid_w
    return pl.pallas_call(
        functools.partial(backward_kernel, comps),
        out_shape=(
            sds((stack_rows, emb), BF16),
            sds((8, hid_w), F32),
            sds((own_rows, feat_w), F32),
        ),
        in_specs=[pl.BlockSpec(memory_space=pltpu.SMEM)] + [vmem] * 8,
        out_specs=(vmem,) * 3,
        scratch_shapes=[pltpu.VMEM((rows, emb), BF16), pltpu.VMEM((n_y * n_z * 16, LANES), BF16)],
        compiler_params=pltpu.CompilerParams(vmem_limit_bytes=56 * 1024 * 1024),
        name="backward",
    )(own, g_all, xc, pre, hid, raw, w_in, w_out, w_gate)


def weights_kernel(n_y, n_z, n_g, stack_ref, gate_ref, in_ref, out_ref, go_ref, x_buf, g_buf, full, *sems):
    core, y, z = place(n_y, n_z)
    dp = lax.axis_index("dp")
    me = item_id(core, y, z, n_y)
    _, y_peers, partner = item_peers(core, y, z, n_y, n_z, dp)
    x_peers = [(me, lax.rem(dp + s, n_g)) for s in range(1, n_g)]
    xs, xr, gs, gr, ys, yr, cs, cr, local = sems
    greet(x_peers + y_peers + [partner])

    copies = []
    for s, (item, group) in enumerate(x_peers):
        copies.append(remote(stack_ref.at[core, y], x_buf.at[dp], xs.at[s], xr.at[s], item, group))
        copies[-1].start()
        copies.append(remote(gate_ref, g_buf.at[dp], gs.at[s], gr.at[s], item, group))
        copies[-1].start()
    mine = pltpu.make_async_copy(stack_ref.at[core, y], x_buf.at[dp], local.at[0])
    mine.start()
    mine_g = pltpu.make_async_copy(gate_ref, g_buf.at[dp], local.at[1])
    mine_g.start()
    mine.wait()
    mine_g.wait()
    for copy in copies:
        copy.wait()
    total = x_buf[0].astype(F32)
    gate = g_buf[0]
    for j in range(1, n_g):
        total = total + x_buf[j].astype(F32)
        gate = gate + g_buf[j]
    full[core, y] = total.astype(BF16)
    go_ref[...] = gate

    copies = []
    for s, (item, _) in enumerate(y_peers):
        block = full.at[core, y]
        copies.append(remote(block, block, ys.at[s], yr.at[s], item, dp))
        copies[-1].start()
    for copy in copies:
        copy.wait()
    block = full.at[core]
    copy = remote(block, block, cs, cr, partner[0], partner[1])
    copy.start()
    copy.wait()

    feat_w, hid_w = in_ref.shape
    emb = out_ref.shape[1]
    span = full.shape[2]
    n_in = feat_w * (hid_w // emb)
    for c in range(2):
        for j in range(n_y):
            at = (c * n_y + j) * span
            value = full[c, j].astype(F32)
            if at < n_in:
                col, row = at // feat_w, at % feat_w
                in_ref[row : row + span, col * emb : (col + 1) * emb] = value
            else:
                out_ref[at - n_in : at - n_in + span, :] = value


def weights(stack, gate, feat_w, hid_w, n_y, n_z, n_g):
    vmem = pl.BlockSpec(memory_space=pltpu.VMEM)
    dma = pltpu.SemaphoreType.DMA
    sds = jax.ShapeDtypeStruct
    span = stack.shape[0] // (2 * n_y)
    emb = stack.shape[1]
    return pl.pallas_call(
        functools.partial(weights_kernel, n_y, n_z, n_g),
        out_shape=(sds((feat_w, hid_w), F32), sds((hid_w, emb), F32), sds(gate.shape, F32)),
        in_specs=[vmem] * 2,
        out_specs=(vmem,) * 3,
        scratch_shapes=[
            pltpu.VMEM((n_g, span, emb), BF16),
            pltpu.VMEM((n_g,) + gate.shape, F32),
            pltpu.VMEM((2, n_y, span, emb), BF16),
            dma((n_g - 1,)),
            dma((n_g - 1,)),
            dma((n_g - 1,)),
            dma((n_g - 1,)),
            dma((n_y - 1,)),
            dma((n_y - 1,)),
            dma(()),
            dma(()),
            dma((2,)),
        ],
        compiler_params=pltpu.CompilerParams(collective_id=2, has_side_effects=True),
        name="weights",
    )(stack.reshape(2, n_y, span, emb), gate)


def per_device(n_y, n_z, n_g, query_feats, positives, query_count, item_table, item_gates, w_in, w_out, w_gate):
    shards = 2 * n_y * n_z
    own_rows, feat_w = query_feats.shape[1:]
    comps = w_gate.shape[1]
    slots = own_rows * shards
    rows = CHUNK * n_y * n_z
    items = item_table.shape[0]

    gathered = gather_rows(query_feats[0], n_y, n_z).reshape(slots, feat_w)

    def by_place(values):
        inner = values.shape[1:]
        order = (2, 1, 0) + tuple(range(3, 3 + len(inner)))
        return values.reshape((n_z, n_y, 2) + inner).transpose(order).reshape(values.shape)

    core, y, z = place(n_y, n_z)
    here = (core * n_y + y) * n_z + z
    counts = by_place(query_count[0])
    index = jnp.arange(shards, dtype=jnp.int32)
    offset = jnp.sum(jnp.where(index[:, None] < index[None, :], counts[:, None], 0), axis=0)
    slot = jnp.arange(own_rows, dtype=jnp.int32)
    ranks = jnp.where(slot[None, :] < counts[:, None], offset[:, None] + slot[None, :], -1).reshape(1, slots)
    pos_local = by_place(positives[0].reshape(shards, own_rows)).reshape(1, slots)
    pos_local = (pos_local - lax.axis_index("item") * items).astype(F32)
    own = jnp.stack(
        [jnp.sum(jnp.where(index == here, offset, 0)), jnp.sum(jnp.where(index == here, counts, 0))]
    )
    gates16 = jnp.concatenate([item_gates] * 4, axis=0)
    w_gate_wide = jnp.pad(w_gate, ((0, 0), (0, LANES - comps)))

    pay, qb, xc, pre, hid, raw = sweep(
        gathered, ranks, pos_local, item_table, gates16, w_in, w_out, w_gate_wide, comps, rows, n_y, n_z
    )
    g_all = reduce_rows(pay, qb, n_y, n_z)
    stack, gate, feats = backward(own, g_all, xc, pre, hid, raw, w_in, w_out, w_gate_wide, comps, own_rows)
    g_in, g_out, g_gate = weights(stack, gate, feat_w, w_in.shape[1], n_y, n_z, n_g)
    return feats.reshape(1, own_rows, feat_w), g_in, g_out, g_gate[:comps].T


def solution(mesh):
    shards = mesh.shape["item"]
    n_y = 4 if shards >= 64 else 2
    n_z = shards // (2 * n_y)
    in_specs = (
        P("dp", "item", None),
        P("dp", None),
        P("dp", None),
        P("item", None),
        P(None, "item"),
        P(),
        P(),
        P(),
    )
    out_specs = (P("dp", "item", None), P(), P(), P())
    return jax.shard_map(
        functools.partial(per_device, n_y, n_z, mesh.shape["dp"]),
        mesh=mesh,
        in_specs=in_specs,
        out_specs=out_specs,
        check_vma=False,
    )
```

time: 916 us -> 126 us (0.14)
  blocking collectives: 547 us -> 0 us
  waiting for transfers between devices: 176 us -> 0 us
  Pallas kernels: 0 us -> 106 us
  matrix products: 79.4 us -> 0 us
  other arithmetic: 51.5 us -> 7.14 us
  local copies, waits for them, and re-layouts: 45 us -> 11.8 us
  between operations: 15 us -> 0.74 us
    unnamed x1 -> x0, blocking collectives: 247 us -> none
    psum x2 -> x0, blocking collectives: 203 us -> none  [the longest x1 124 us: per_device(): totals_all = lax.psum(totals, 'item')]
    psum x1 -> x0, waiting for transfers between devices: 176 us -> none  [per_device(): lax.psum((part_in, part_out, part_gate), ('item', 'dp'))]
    pallas_call x0 -> x5, Pallas kernels: none -> 106 us  [the longest x1 31.6 us: reduce_rows(): pl.pallas_call(functools.partial(reduce_kernel, n_y, n_z), out_shape=jax....]
    all_gather x2 -> x0, blocking collectives: 97.7 us -> none  [the longest x1 54.9 us: per_device(): lax.all_gather(query_norm, 'item', axis=0, tiled=True)]
    dot_general x25 -> x0, matrix products: 79.4 us -> none  [the longest x8 41.9 us: one_block(): jnp.einsum('kri,ikd->rkd', coef_bf, item_part, preferred_element_type=jnp...]
    reduce_sum x22 -> x3, other arithmetic: 38 us -> 1.39 us  [the longest x1 0.66 us: per_device(): jnp.sum(jnp.where(index == here, counts, 0))]
    gather x4 -> x0, local copies, waits for them, and re-layouts: 12 us -> none  [the longest x2 6.37 us: positive_terms(): item_pos = jnp.take(item_norm, safe_id, axis=0).astype(jnp.float32)]
  transfers between devices with their start and end apart: 2 -> 0, of which waited for: 1 -> 0; matrix products, arithmetic and copies ran while one was open for 0% -> 0% of each run, Pallas kernels for 0% -> 0%
where the time goes in v1:
time: 126 us
  Pallas kernels  106 us (84%)
  local copies, waits for them, and re-layouts  11.8 us (9%)
  other arithmetic  7.14 us (6%)
    pallas_call x1, Pallas kernels, reduce_rows(): pl.pallas_call(functools.partial(reduce_kernel, n_y, n_z), out_shape=jax....  31.6 us
    pallas_call x1, Pallas kernels, sweep(): pl.pallas_call(functools.partial(sweep_kernel, comps), out_shape=(sds((2,...  27.1 us
    pallas_call x1, Pallas kernels, gather_rows(): pl.pallas_call(functools.partial(gather_kernel, n_y, n_z), out_shape=jax....  21.4 us
    pallas_call x1, Pallas kernels, weights(): pl.pallas_call(functools.partial(weights_kernel, n_y, n_z, n_g), out_shap...  17.7 us
    pallas_call x1, Pallas kernels, backward(): pl.pallas_call(functools.partial(backward_kernel, comps), out_shape=(sds(...  8.32 us
    unnamed x10, local copies, waits for them, and re-layouts  8.07 us

profile of v1, /device:TPU:1, one launch (start us, length us, event | category | flops | bytes accessed | tf_op | source)
XLA Modules:
  0.0 125.8 jit_solution(15245058175815583832)
XLA Ops:
  0.7 0.5 broadcast.48
  1.2 1.3 %reduce.8 = s32[64]{0:T(128)S(1)} reduce(s32[1,64]{1,0:T(1,128)} %param.10, s32[]{:T(128)} %broadcast.48), dimensions={0}, to_apply=%param.10.reduce_sub_computation.3 | reduce | bytes 516 | tf_op args[2]
  2.5 0.7 convert_reduce_fusion
  3.2 0.1 reshape_squeeze.3
  3.3 0.7 select_reduce_fusion.1
  4.0 0.1 copy.18
  4.3 0.6 fusion
  4.9 1.9 %pad_add_fusion.own_ref = s32[2]{0:T(128)} fusion(s32[1]{0:T(128)} %bitcast.2, s32[1]{0:T(128)} %bitcast.1), kind=kLoop, calls=%fused_computation.12 | loop fusion | flops 2 | bytes 16 | tf_op jit(solution)/shard_map/stack | solution.py:659
  6.9 0.7 convert_element_type.14.pos_ref
  7.7 0.7 select_n.40.rank_ref
  8.4 0.9 copy.20
  9.2 0.7 pad.4.w_gate_ref
  9.9 1.8 %pad_maximum_fusion.gate_ref = f32[16,4096]{1,0:T(8,128)} fusion(f32[4,4096]{1,0:T(4,128)} %param.12), kind=kLoop, calls=%fused_computation | loop fusion | flops 196608 | bytes 327680 | tf_op jit(solution)/shard_map/concatenate | solution.py:662
  11.7 21.4 %gather_rows.1 = bf16[2,4,8,16,256]{4,3,2,1,0:T(8,128)(2,1)} custom-call(bf16[16,256]{1,0:T(8,128)(2,1)} %bitcast.19), custom_call_target="tpu_custom_call" | custom-call | tf_op jit(solution)/shard_map/gather_rows/pallas_call | solution.py:156
  33.1 27.1 %sweep.1 = (bf16[2,4,8,56,128]{4,3,2,1,0:T(8,128)(2,1)}, bf16[2,4,8,24,128]{4,3,2,1,0:T(8,128)(2,1)}, bf16[768,256]{1,0:T(8,128)(2,1)}, f32[768,512]{1,0:T(8,128...) custom-call(bf16[1024,256]{1,0:T(8,128)(2,1)} %bitcast.15, s32[1,1024]{1,0:T(1,128)} %select_n.40.rank_ref, ...), custom_call_target="tpu_custom_call" | custom-call | tf_op jit(solution)/shard_map/sweep/pallas_call | solution.py:333
  60.2 1.2 copy-done.1
  61.4 1.0 copy-done.2
  62.4 31.6 %reduce_rows.1.g_ref = bf16[2,4,8,32,128]{4,3,2,1,0:T(8,128)(2,1)S(1)} custom-call(bf16[2,4,8,56,128]{4,3,2,1,0:T(8,128)(2,1)S(1)} %copy-done.1, bf16[2,4,8,24,128]{4,3,2,1,0:T(8,128)(2,1)S(1)} %copy-done.2), custom_call_target="tpu_custom_call" | custom-call | tf_op jit(solution)/shard_map/reduce_rows/pallas_call | solution.py:427
  94.0 0.8 copy-done
  94.8 8.3 %backward.1 = (bf16[1024,256]{1,0:T(8,128)(2,1)}, f32[8,512]{1,0:T(8,128)}, f32[16,256]{1,0:T(8,128)}) custom-call(s32[2]{0:T(128)} %pad_add_fusion.own_ref, bf16[2,4,8,32,128]{4,3,2,1,0:T(8,128)(2,1)} %copy-done, bf16[768,256]{1,0:T(8,128)(2,1)} %get-tuple-element.18.xc_ref, f32[768,512]{1,0:T(8,128)} %get-tuple-element.19.pre_ref, ...), custom_call_target="tpu_custom_call" | custom-call | tf_op jit(solution)/shard_map/backward/pallas_call | solution.py:532
  103.1 17.7 %weights.1 = (f32[256,512]{1,0:T(8,128)}, f32[512,256]{1,0:T(8,128)}, f32[8,512]{1,0:T(8,128)}) custom-call(bf16[2,4,128,256]{3,2,1,0:T(8,128)(2,1)} %bitcast.16, f32[8,512]{1,0:T(8,128)} %get-tuple-element.24.gate_ref), custom_call_target="tpu_custom_call" | custom-call | tf_op jit(solution)/shard_map/weights/pallas_call | solution.py:611
  120.8 1.3 %slice_bitcast_fusion = f32[512,4]{0,1:T(4,128)} fusion(f32[8,512]{1,0:T(8,128)} %get-tuple-element.27), kind=kLoop, calls=%fused_computation.8 | loop fusion | bytes 16384 | tf_op jit(solution)/shard_map/transpose | solution.py:671
  122.1 1.9 %copy.25 = f32[256,512]{1,0:T(8,128)} copy(f32[256,512]{1,0:T(8,128)} %get-tuple-element.33) | data formatting | bytes 1048576
  124.0 1.9 %copy.26 = f32[512,256]{1,0:T(8,128)} copy(f32[512,256]{1,0:T(8,128)} %get-tuple-element.34) | data formatting | bytes 1048576
  (8 shorter events, 0.4 us)
Async XLA Ops:
  60.2 1.2 copy-start.1
  61.4 1.0 copy-start.2
  94.0 0.8 copy-start
